TPU v7x, 128 devices: a whole 4x4x4 slice. The times are simulated.
128 devices in a mesh: cand: 4 (over x_lo, core), seq: 32 (over x_hi, y, z).
Axes of the slice: x: 4 (x_hi: 2, x_lo: 2; x = x_hi * 2 + x_lo), y: 4, z: 4, core: 2. Of those that a mesh axis runs over, the one named last changes fastest.
Arguments:
- hyena_query: bfloat16 [4, 4096, 4096], P('cand', 'seq'), may hold values from -6 to 6
- hyena_key: bfloat16 [4, 4096, 4096], P('cand', 'seq'), may hold values from -6 to 6
- hyena_value: bfloat16 [4, 4096, 4096], P('cand', 'seq'), may hold values from -6 to 6
- hyena_filters: float32 [128, 256], replicated, may hold values from -0.5 to 0.5
- context_tail: bfloat16 [127, 4096], replicated, may hold values from -6 to 6
- cont_queries: bfloat16 [4, 4096, 32, 128], P('cand', 'seq'), may hold values from -100 to 100
- cont_keys: bfloat16 [4, 4096, 32, 128], P('cand', 'seq'), may hold values from -5 to 5
- cont_values: bfloat16 [4, 4096, 32, 128], P('cand', 'seq'), may hold values from -6 to 6
- context_keys: bfloat16 [3072, 32, 128], P('seq'), may hold values from -6 to 6
- context_values: bfloat16 [3072, 32, 128], P('seq'), may hold values from -6 to 6
- lengths: int32 [4], P('cand'), may hold values from 1024 to 4096, as said below
Outputs:
- hyena_out: bfloat16 [4, 4096, 4096], P('cand', 'seq')
- attention_out: bfloat16 [4, 4096, 32, 128], P('cand', 'seq')
Inputs may be any that keep to these rules, and one draw needn't show every extreme that they name: `lengths`: positions of a candidate at or past its length are padding; some candidate has all 4096 positions valid.
All inputs are finite; a program needn't handle non-finite values.
Results may differ from a plain program's by a relative error of at most 0.0049.
Values may be sent and summed in bfloat16 or wider, within the bound.
A program may use at most 64 MiB of HBM per device.

v0:
```python
import math

import jax
import jax.numpy as jnp
from jax import lax
from jax.sharding import PartitionSpec as P

CH_GROUP = 16


masked_score = -1e30


def shifted(x, axis, by):
    peers = lax.axis_size(axis)
    pairs = [(i, i + by) for i in range(peers) if 0 <= i + by < peers]
    return lax.ppermute(x, axis, pairs)


def merge_scores(carried, scores, value_rows):
    run_max, run_total, weighted = carried
    new_max = jnp.maximum(run_max, jnp.max(scores, axis=-1))
    weights = jnp.exp(scores - new_max[..., None])
    shrink = jnp.exp(run_max - new_max)
    new_total = run_total * shrink + jnp.sum(weights, axis=-1)
    mixed = jnp.einsum(
        "hqk,khd->hqd", weights.astype(jnp.bfloat16), value_rows, preferred_element_type=jnp.float32
    )
    return (new_max, new_total, weighted * shrink[..., None] + mixed)


def fold_context(carried, queries, key_rows, value_rows):
    scaling = 1.0 / math.sqrt(queries.shape[-1])

    def per_block(operands):
        run_max, run_total, weighted, query_block = operands
        scores = (
            jnp.einsum("hqd,khd->hqk", query_block, key_rows, preferred_element_type=jnp.float32)
            * scaling
        )
        return merge_scores((run_max, run_total, weighted), scores, value_rows)

    return lax.map(per_block, (carried[0], carried[1], carried[2], queries))


def fold_own(carried, queries, key_rows, value_rows):
    scaling = 1.0 / math.sqrt(queries.shape[-1])
    block_rows = queries.shape[2]
    key_places = jnp.arange(key_rows.shape[0])

    def per_block(operands):
        run_max, run_total, weighted, query_block, index = operands
        query_places = index * block_rows + jnp.arange(block_rows)
        scores = (
            jnp.einsum("hqd,khd->hqk", query_block, key_rows, preferred_element_type=jnp.float32)
            * scaling
        )
        allowed = key_places[None, :] <= query_places[:, None]
        scores = jnp.where(allowed[None], scores, masked_score)
        return merge_scores((run_max, run_total, weighted), scores, value_rows)

    return lax.map(
        per_block, (carried[0], carried[1], carried[2], queries, jnp.arange(queries.shape[0]))
    )


def local(
    hyena_query,
    hyena_key,
    hyena_value,
    hyena_filters,
    context_tail,
    cont_queries,
    cont_keys,
    cont_values,
    context_keys,
    context_values,
    lengths,
):
    rows = hyena_key.shape[1]
    taps = hyena_filters.shape[0]
    product = (hyena_key.astype(jnp.float32) * hyena_value.astype(jnp.float32)).astype(jnp.bfloat16)
    received = shifted(product[:, rows - (taps - 1) :, :], "seq", 1)
    is_first = lax.axis_index("seq") == 0
    earlier = jnp.where(is_first, context_tail[None], received)
    extended = jnp.concatenate([earlier, product], axis=1).astype(jnp.float32)
    per_channel = jnp.repeat(hyena_filters, CH_GROUP, axis=1)
    kernel = per_channel[::-1][:, None, :]
    convolved = lax.conv_general_dilated(
        extended,
        kernel,
        (1,),
        "VALID",
        dimension_numbers=("NWC", "WIO", "NWC"),
        feature_group_count=extended.shape[2],
        precision=lax.Precision.HIGHEST,
    )
    places = lax.axis_index("seq") * rows + jnp.arange(rows)
    keep = places[None, :] < lengths[:, None]
    hyena_out = jnp.where(
        keep[:, :, None], hyena_query.astype(jnp.float32) * convolved, 0.0
    ).astype(jnp.bfloat16)
    shared_keys, shared_values = (
        lax.all_to_all(context_keys, "seq", split_axis=1, concat_axis=0, tiled=True),
        lax.all_to_all(context_values, "seq", split_axis=1, concat_axis=0, tiled=True),
    )

    def single(operands):
        query_rows, key_rows, value_rows = operands
        length_all, heads_local, width = query_rows.shape
        block_rows = min(512, length_all)
        count = length_all // block_rows
        queries = query_rows.reshape(count, block_rows, heads_local, width).transpose(0, 2, 1, 3)
        carried = (
            jnp.full((count, heads_local, block_rows), masked_score, jnp.float32),
            jnp.zeros((count, heads_local, block_rows), jnp.float32),
            jnp.zeros((count, heads_local, block_rows, width), jnp.float32),
        )
        carried = fold_context(carried, queries, shared_keys, shared_values)
        carried = fold_own(carried, queries, key_rows, value_rows)
        result = carried[2] / carried[1][..., None]
        return (
            result.transpose(0, 2, 1, 3)
            .reshape(length_all, heads_local, width)
            .astype(jnp.bfloat16)
        )

    attended = lax.map(
        single,
        (
            lax.all_to_all(cont_queries, "seq", split_axis=2, concat_axis=1, tiled=True),
            lax.all_to_all(cont_keys, "seq", split_axis=2, concat_axis=1, tiled=True),
            lax.all_to_all(cont_values, "seq", split_axis=2, concat_axis=1, tiled=True),
        ),
    )
    attention = lax.all_to_all(attended, "seq", split_axis=1, concat_axis=2, tiled=True)
    attention_out = jnp.where(keep[:, :, None, None], attention, jnp.zeros((), jnp.bfloat16))
    return (hyena_out, attention_out)


def solution(mesh):
    placed = (
        P("cand", "seq", None),
        P("cand", "seq", None),
        P("cand", "seq", None),
        P(),
        P(),
        P("cand", "seq", None, None),
        P("cand", "seq", None, None),
        P("cand", "seq", None, None),
        P("seq", None, None),
        P("seq", None, None),
        P("cand"),
    )
    return jax.shard_map(
        local,
        mesh=mesh,
        in_specs=placed,
        out_specs=(P("cand", "seq", None), P("cand", "seq", None, None)),
        check_vma=False,
    )
```

profile of v0, /device:TPU:8, one launch (start us, length us, event | category | flops | bytes accessed | tf_op | source)
XLA Modules:
  0.0 309.6 jit_solution(5731969124352220788)
XLA Ops:
  0.6 2.4 copy.76
  3.0 11.1 %all-to-all-start.1 = ((bf16[96,32,128]{2,0,1:T(8,128)(2,1)}), bf16[96,32,128]{2,0,1:T(8,128)(2,1)S(1)}, u32[]{:S(2)}, u32[]{:S(2)}) async-start(bf16[96,32,128]{2,0,1:T(8,128)(2,1)} %copy.76), calls=%async_computation.1 | async-start | bytes 1572864 | tf_op jit(solution)/shard_map/all_to_all | solution.py:104
  15.4 13.1 %all-to-all-done.1 = bf16[96,32,128]{2,0,1:T(8,128)(2,1)S(1)} async-done(((bf16[96,32,128]{2,0,1:T(8,128)(2,1)}), bf16[96,32,128]{2,0,1:T(8,128)(2,1)S(1)}, u32[]{:S(2)}, u32[]{:S(2)}) %all-to-all-start.1) | async-done | bytes 786464 | tf_op jit(solution)/shard_map/all_to_all | solution.py:104
  28.4 5.9 %all-to-all-start.2 = ((bf16[96,32,128]{2,0,1:T(8,128)(2,1)}), bf16[96,32,128]{2,0,1:T(8,128)(2,1)S(1)}, u32[]{:S(2)}, u32[]{:S(2)}) async-start(bf16[96,32,128]{2,0,1:T(8,128)(2,1)} %copy.77), calls=%async_computation.2 | async-start | bytes 1572864 | tf_op jit(solution)/shard_map/all_to_all | solution.py:105
  35.7 11.4 %all-to-all-done.2 = bf16[96,32,128]{2,0,1:T(8,128)(2,1)S(1)} async-done(((bf16[96,32,128]{2,0,1:T(8,128)(2,1)}), bf16[96,32,128]{2,0,1:T(8,128)(2,1)S(1)}, u32[]{:S(2)}, u32[]{:S(2)}) %all-to-all-start.2) | async-done | bytes 786464 | tf_op jit(solution)/shard_map/all_to_all | solution.py:105
  47.1 5.9 %all-to-all-start = ((bf16[1,128,32,128]{3,1,0,2:T(8,128)(2,1)}), bf16[1,128,32,128]{3,1,0,2:T(8,128)(2,1)S(1)}, u32[]{:S(2)}, u32[]{:S(2)}) async-start(bf16[1,128,32,128]{3,1,0,2:T(8,128)(2,1)} %copy.75), calls=%async_computation | async-start | bytes 2097152 | tf_op jit(solution)/shard_map/all_to_all | solution.py:131
  53.0 2.7 copy.79
  55.7 11.4 %all-to-all-done = bf16[1,128,32,128]{3,1,0,2:T(8,128)(2,1)S(1)} async-done(((bf16[1,128,32,128]{3,1,0,2:T(8,128)(2,1)}), bf16[1,128,32,128]{3,1,0,2:T(8,128)(2,1)S(1)}, u32[]{:S(2)}, u32[]{:S(2)}) %all-to-all-start) | async-done | bytes 1048608 | tf_op jit(solution)/shard_map/all_to_all | solution.py:131
  67.1 6.2 %all-to-all-start.3 = ((bf16[1,128,32,128]{3,1,0,2:T(8,128)(2,1)}), bf16[1,128,32,128]{3,1,0,2:T(8,128)(2,1)}, u32[]{:S(2)}, u32[]{:S(2)}) async-start(bf16[1,128,32,128]{3,1,0,2:T(8,128)(2,1)} %copy.79), calls=%async_computation.3 | async-start | bytes 2097152 | tf_op jit(solution)/shard_map/all_to_all | solution.py:132
  77.3 3.4 %collective-permute-start = (bf16[1,127,4096]{2,1,0:T(8,128)(2,1)}, bf16[1,127,4096]{2,1,0:T(8,128)(2,1)}, u32[]{:S(2)}, u32[]{:S(2)}) collective-permute-start(bf16[1,127,4096]{2,1,0:T(8,128)(2,1)} %slice.4), channel_id=1, source_target_pairs={{0,1},{1,2},{2,3},{3,4},{4,5},{5,6},{6,7},{7,8},{8,9},{9,10},{10,1... | collective-permute-start | bytes 3121160 | tf_op jit(solution)/shard_map/ppermute | solution.py:17
  80.7 2.6 copy.80
  85.6 17.5 %rev.3 = f32[128,4096]{0,1:T(8,128)} reverse(f32[128,4096]{0,1:T(8,128)} %bitcast.133), dimensions={0} | reverse | bytes 4194304 | tf_op jit(solution)/shard_map/rev | solution.py:88
  103.0 5.7 %copy.74 = f32[128,1,4096]{2,1,0:T(1,128)} copy(f32[128,1,4096]{0,2,1:T(8,128)} %bitcast.134) | data formatting | bytes 4194304 | tf_op jit(solution)/shard_map/broadcast_in_dim | solution.py:88
  108.7 9.6 %all-to-all-start.4 = ((bf16[1,128,32,128]{3,1,0,2:T(8,128)(2,1)}), bf16[1,128,32,128]{3,1,0,2:T(8,128)(2,1)S(1)}, u32[]{:S(2)}, u32[]{:S(2)}) async-start(bf16[1,128,32,128]{3,1,0,2:T(8,128)(2,1)} %copy.80), calls=%async_computation.4 | async-start | bytes 2097152 | tf_op jit(solution)/shard_map/all_to_all | solution.py:133
  119.8 41.4 %while.40 = (s32[]{:T(128)}, f32[8,1,512]{2,1,0:T(1,128)S(1)}, f32[8,1,512]{2,1,0:T(1,128)S(1)}, f32[8,1,512,128]{3,2,1,0:T(8,128)}, bf16[8,1,512,128]{3,2,1,0:T...) while((s32[]{:T(128)}, f32[8,1,512]{2,1,0:T(1,128)S(1)}, ...), condition=%wide.region_3.4_spmd, body=%wide.region_0.3_spmd.sunk | while | flops 817956864 | bytes 20866136 | solution.py:43
  121.8 2.0 fusion.66
  126.9 2.0 fusion.66
  130.1 2.0 multiply_reduce_fusion.2
  132.1 2.0 fusion.66
  135.3 2.0 multiply_reduce_fusion.2
  137.3 2.0 fusion.66
  142.4 2.0 fusion.66
  145.6 2.0 multiply_reduce_fusion.2
  147.6 2.0 fusion.66
  152.8 2.0 fusion.66
  158.0 2.0 fusion.66
  161.3 63.6 %while.41 = (s32[]{:T(128)}, f32[8,1,512]{2,0,1:T(8,128)S(1)}, f32[8,1,512,128]{3,2,1,0:T(8,128)S(1)}, f32[8,1,512]{2,1,0:T(1,128)S(1)}, f32[8,1,512]{2,1,0:T(1,...) while((s32[]{:T(128)}, f32[8,1,512]{2,0,1:T(8,128)S(1)}, ...), condition=%wide.region_7.8_spmd.clone, body=%wide.region_4.7_spmd.clone.sunk | while | flops 1090652672 | bytes 27959976 | solution.py:62
  162.4 3.0 fusion.69
  165.5 2.4 fusion.71
  170.4 3.0 fusion.69
  173.4 2.4 fusion.71
  178.3 3.0 fusion.69
  181.4 2.4 fusion.71
  186.3 3.0 fusion.69
  189.3 2.4 fusion.71
  194.2 3.0 fusion.69
  197.3 2.4 fusion.71
  202.2 3.0 fusion.69
  205.2 2.4 fusion.71
  210.2 3.0 fusion.69
  213.2 2.4 fusion.71
  218.1 3.0 fusion.69
  221.2 2.4 fusion.71
  225.7 16.7 %copy.100 = bf16[1,4096,1,128]{3,2,0,1:T(2,128)(2,1)S(1)} copy(bf16[1,4096,1,128]{3,1,2,0:T(8,128)(2,1)S(1)} %bitcast.135) | data formatting | bytes 2097152 | tf_op jit(solution)/shard_map/while/body/eval_jaxpr/convert_element_type | solution.py:125
  243.0 22.6 %reduce.8 = bf16[4096,128]{1,0:T(8,128)(2,1)S(1)} reduce(bf16[4096,1,1,128]{3,2,1,0:T(2,128)(2,1)S(1)} %bitcast.132, bf16[]{:T(256)} %broadcast.150), dimensions={1,2}, to_apply=%bitcast.94.reduce_sub_computation | reduce | bytes 2097154
  266.7 9.8 %all-to-all-start.5 = ((bf16[32,2,8192]{2,1,0:T(2,128)(2,1)}), bf16[32,2,8192]{2,1,0:T(2,128)(2,1)S(1)}, u32[]{:S(2)}, u32[]{:S(2)}) async-start(bf16[32,2,8192]{2,1,0:T(2,128)(2,1)} %reshape.221), calls=%async_computation.5 | async-start | bytes 2097152 | tf_op jit(solution)/shard_map/all_to_all | solution.py:136
  279.9 24.6 %fusion.48 = bf16[1,128,4096]{2,0,1:T(2,128)(2,1)S(1)} fusion(f32[128,1,4096]{2,1,0:T(1,128)S(1)} %copy-done.3, bf16[1,255,4096]{2,1,0:T(8,128)(2,1)S(1)} %pad_maximum_fusion, pred[128]{0:T(512)(128)(4,1)S(1)} %add_compare_fusion, bf16[1,128,4096]{2,1,0:T(8,128)(2,1)S(1)} %copy-done.8), kind=kOutput, calls=%fused_computation.48 | convolution fusion | flops 807403520 | bytes 6283392 | tf_op jit(solution)/shard_map/conv_general_dilated | solution.py:89
  304.5 2.1 copy.84
  (129 shorter events, 53.3 us)
Async XLA Ops:
  0.6 13.6 %copy-start.6 = (bf16[96,32,128]{2,1,0:T(8,128)(2,1)S(1)}, bf16[96,32,128]{2,1,0:T(8,128)(2,1)}, u32[]{:S(2)}) copy-start(bf16[96,32,128]{2,1,0:T(8,128)(2,1)} %param.24) | copy-start | bytes 2359300
  3.0 31.3 %copy-start.4 = (bf16[1,128,32,128]{3,2,1,0:T(8,128)(2,1)S(1)}, bf16[1,128,32,128]{3,2,1,0:T(8,128)(2,1)}, u32[]{:S(2)}) copy-start(bf16[1,128,32,128]{3,2,1,0:T(8,128)(2,1)} %param.20) | copy-start | bytes 3145732
  3.0 25.4 %all-to-all-start.1 = ((bf16[96,32,128]{2,0,1:T(8,128)(2,1)}), bf16[96,32,128]{2,0,1:T(8,128)(2,1)S(1)}, u32[]{:S(2)}, u32[]{:S(2)}) async-start(bf16[96,32,128]{2,0,1:T(8,128)(2,1)} %copy.76), calls=%async_computation.1 | async-start | bytes 1572864 | tf_op jit(solution)/shard_map/all_to_all | solution.py:104
  28.4 18.6 %all-to-all-start.2 = ((bf16[96,32,128]{2,0,1:T(8,128)(2,1)}), bf16[96,32,128]{2,0,1:T(8,128)(2,1)S(1)}, u32[]{:S(2)}, u32[]{:S(2)}) async-start(bf16[96,32,128]{2,0,1:T(8,128)(2,1)} %copy.77), calls=%async_computation.2 | async-start | bytes 1572864 | tf_op jit(solution)/shard_map/all_to_all | solution.py:105
  47.1 20.0 %all-to-all-start = ((bf16[1,128,32,128]{3,1,0,2:T(8,128)(2,1)}), bf16[1,128,32,128]{3,1,0,2:T(8,128)(2,1)S(1)}, u32[]{:S(2)}, u32[]{:S(2)}) async-start(bf16[1,128,32,128]{3,1,0,2:T(8,128)(2,1)} %copy.75), calls=%async_computation | async-start | bytes 2097152 | tf_op jit(solution)/shard_map/all_to_all | solution.py:131
  67.1 8.0 %copy-start.2 = (bf16[1,128,32,128]{3,1,0,2:T(8,128)(2,1)}, bf16[1,128,32,128]{3,1,0,2:T(8,128)(2,1)S(1)}, u32[]{:S(2)}) copy-start(bf16[1,128,32,128]{3,1,0,2:T(8,128)(2,1)S(1)} %all-to-all-done) | copy-start | bytes 3145732
  67.1 41.6 %all-to-all-start.3 = ((bf16[1,128,32,128]{3,1,0,2:T(8,128)(2,1)}), bf16[1,128,32,128]{3,1,0,2:T(8,128)(2,1)}, u32[]{:S(2)}, u32[]{:S(2)}) async-start(bf16[1,128,32,128]{3,1,0,2:T(8,128)(2,1)} %copy.79), calls=%async_computation.3 | async-start | bytes 2097152 | tf_op jit(solution)/shard_map/all_to_all | solution.py:132
  75.1 1.0 copy-start
  76.0 7.9 %copy-start.7 = (f32[128,256]{1,0:T(8,128)S(1)}, f32[128,256]{1,0:T(8,128)}, u32[]{:S(2)}) copy-start(f32[128,256]{1,0:T(8,128)} %param.18) | copy-start | bytes 393220
  77.3 199.2 %collective-permute-start = (bf16[1,127,4096]{2,1,0:T(8,128)(2,1)}, bf16[1,127,4096]{2,1,0:T(8,128)(2,1)}, u32[]{:S(2)}, u32[]{:S(2)}) collective-permute-start(bf16[1,127,4096]{2,1,0:T(8,128)(2,1)} %slice.4), channel_id=1, source_target_pairs={{0,1},{1,2},{2,3},{3,4},{4,5},{5,6},{6,7},{7,8},{8,9},{9,10},{10,1... | collective-permute-start | bytes 3121160 | tf_op jit(solution)/shard_map/ppermute | solution.py:17
  108.7 52.4 %all-to-all-start.4 = ((bf16[1,128,32,128]{3,1,0,2:T(8,128)(2,1)}), bf16[1,128,32,128]{3,1,0,2:T(8,128)(2,1)S(1)}, u32[]{:S(2)}, u32[]{:S(2)}) async-start(bf16[1,128,32,128]{3,1,0,2:T(8,128)(2,1)} %copy.80), calls=%async_computation.4 | async-start | bytes 2097152 | tf_op jit(solution)/shard_map/all_to_all | solution.py:133
  265.5 11.0 %copy-start.5 = (bf16[127,4096]{1,0:T(8,128)(2,1)S(1)}, bf16[127,4096]{1,0:T(8,128)(2,1)}, u32[]{:S(2)}) copy-start(bf16[127,4096]{1,0:T(8,128)(2,1)} %param.19) | copy-start | bytes 3121156
  266.7 39.9 %all-to-all-start.5 = ((bf16[32,2,8192]{2,1,0:T(2,128)(2,1)}), bf16[32,2,8192]{2,1,0:T(2,128)(2,1)S(1)}, u32[]{:S(2)}, u32[]{:S(2)}) async-start(bf16[32,2,8192]{2,1,0:T(2,128)(2,1)} %reshape.221), calls=%async_computation.5 | async-start | bytes 2097152 | tf_op jit(solution)/shard_map/all_to_all | solution.py:136
  276.5 1.5 copy-start.1
  278.0 1.6 copy-start.3
  278.0 1.9 copy-start.8
where the time goes:
time: 313 us; the launch traced here: 310 us
  matrix products  99.5 us (32%)
  local copies, waits for them, and re-layouts  68.8 us (22%)
  starting transfers between devices  51.8 us (17%)
  other arithmetic  47 us (15%)
  waiting for transfers between devices  35.9 us (11%)
  loops' own time  5.03 us (2%)
    dot_general x16, matrix products, per_block(): jnp.einsum('hqd,khd->hqk', query_block, key_rows, preferred_element_type=...  39.9 us
    dot_general x16, matrix products, merge_scores(): jnp.einsum('hqk,khd->hqd', weights.astype(jnp.bfloat16), value_rows, pref...  35.1 us
    conv_general_dilated x1, matrix products, local(): lax.conv_general_dilated(extended, kernel, (1,), 'VALID', dimension_numbe...  24.6 us
    unnamed x1, other arithmetic  22.6 us
    unnamed x30, local copies, waits for them, and re-layouts  19.6 us
    reduce_sum x16, other arithmetic, merge_scores(): new_total = run_total * shrink + jnp.sum(weights, axis=-1)  19.5 us
    rev x1, local copies, waits for them, and re-layouts, local(): kernel = per_channel[::-1][:, None, :]  17.5 us
    convert_element_type x1, local copies, waits for them, and re-layouts, single(): return result.transpose(0, 2, 1, 3).reshape(length_all, heads_local, widt...  16.7 us
  transfers between devices with their start and end apart: 7, of which 3 were waited for; matrix products, arithmetic and copies ran while one was open for 67% of the time, Pallas kernels for 0%

commit v1 on v0

v1 whole, which is shorter than its diff:
```python
import functools
import math

import jax
import jax.numpy as jnp
from jax import lax
from jax.experimental import pallas as pl
from jax.experimental.pallas import tpu as pltpu
from jax.sharding import PartitionSpec as P

F32 = jnp.float32
BF16 = jnp.bfloat16
MESH = pl.DeviceIdType.MESH
NT = (((1,), (1,)), ((), ()))
NN = (((1,), (0,)), ((), ()))
TN = (((0,), (0,)), ((), ()))
LOW = -1e30


def dot(a, b, dims):
    return lax.dot_general(a, b, dims, preferred_element_type=F32)


def fused(
    n, groups_per_tile, scale,
    hq_hbm, hk_hbm, hv_hbm, filt_ref, tail_hbm, q_hbm, k_hbm, v_hbm, ck_hbm, cv_hbm, len_ref,
    hy_ref, att_ref,
    hq, hk, hv, tail, ext, ring,
    q_in, k_in, v_in, ck_in, cv_in, wide,
    q_out, k_out, v_out, ck_out, cv_out,
    q_all, k_all, v_all, ck_all, cv_all,
    m_s, l_s, acc_s, o_out, o_in,
    load_sem, send_sem, recv_sem,
):
    rows, heads, width = q_in.shape
    half_rows = ck_in.shape[0]
    length_all = n * rows
    me = lax.axis_index("seq")
    cand = lax.axis_index("cand")
    half = lax.rem(cand, 2)
    partner = cand + 1 - 2 * half

    barrier = pltpu.get_barrier_semaphore()

    def greet(i, _):
        pl.semaphore_signal(
            barrier, inc=1, device_id=(cand, lax.rem(me + i, n)), device_id_type=MESH
        )
        return 0

    lax.fori_loop(1, n, greet, 0)
    pl.semaphore_signal(barrier, inc=1, device_id=(partner, me), device_id_type=MESH)

    ctx_rows = pl.ds(half * half_rows, half_rows)
    loads = [
        pltpu.make_async_copy(ck_hbm.at[ctx_rows], ck_in, load_sem.at[0]),
        pltpu.make_async_copy(cv_hbm.at[ctx_rows], cv_in, load_sem.at[1]),
        pltpu.make_async_copy(q_hbm.at[0], q_in, load_sem.at[2]),
        pltpu.make_async_copy(k_hbm.at[0], k_in, load_sem.at[3]),
        pltpu.make_async_copy(v_hbm.at[0], v_in, load_sem.at[4]),
        pltpu.make_async_copy(hk_hbm.at[0], hk, load_sem.at[5]),
        pltpu.make_async_copy(hv_hbm.at[0], hv, load_sem.at[6]),
        pltpu.make_async_copy(hq_hbm.at[0], hq, load_sem.at[7]),
        pltpu.make_async_copy(tail_hbm, tail, load_sem.at[8]),
    ]
    for copy in loads:
        copy.start()

    def by_head(src, dst):
        count = src.shape[0]
        wide[: count * heads, :] = src[...].astype(F32).reshape(count * heads, width)
        for h in range(heads):
            dst[h] = wide[pl.ds(h, count, stride=heads), :].astype(BF16)

    def scatter(src, dst_at, index):
        own = pltpu.make_async_copy(src.at[me], dst_at(me), recv_sem.at[index])
        own.start()

        def send(i, _):
            p = lax.rem(me + i, n)
            pltpu.make_async_remote_copy(
                src_ref=src.at[p], dst_ref=dst_at(me), send_sem=send_sem.at[index],
                recv_sem=recv_sem.at[index], device_id=(cand, p), device_id_type=MESH,
            ).start()
            return 0

        lax.fori_loop(1, n, send, 0)

    def received(whole, index):
        pltpu.make_async_copy(whole, whole, recv_sem.at[index]).wait()

    def sent(part, index):
        pltpu.make_async_copy(part, part, send_sem.at[index]).wait()

    loads[0].wait()
    by_head(ck_in, ck_out)
    loads[1].wait()
    by_head(cv_in, cv_out)
    pl.semaphore_wait(barrier, n)
    scatter(ck_out, lambda s: ck_all.at[half, s], 0)
    scatter(cv_out, lambda s: cv_all.at[half, s], 1)
    loads[2].wait()
    by_head(q_in, q_out)
    scatter(q_out, lambda s: q_all.at[s], 2)
    loads[3].wait()
    by_head(k_in, k_out)
    scatter(k_out, lambda s: k_all.at[s], 3)
    loads[4].wait()
    by_head(v_in, v_out)
    scatter(v_out, lambda s: v_all.at[s], 4)

    loads[5].wait()
    loads[6].wait()
    ext[1] = (hk[...].astype(F32) * hv[...].astype(F32)).astype(BF16)

    def halo(to):
        return pltpu.make_async_remote_copy(
            src_ref=ext.at[1], dst_ref=ext.at[0], send_sem=send_sem.at[5],
            recv_sem=recv_sem.at[5], device_id=(cand, to), device_id_type=MESH,
        )

    @pl.when(me + 1 < n)
    def _():
        halo(me + 1).start()

    loads[8].wait()

    taps = filt_ref.shape[0]
    turn_s = lax.broadcasted_iota(jnp.int32, (taps, taps), 0)
    turn_w = lax.broadcasted_iota(jnp.int32, (taps, taps), 1)
    turned = jnp.where((turn_s + turn_w) % taps == 0, 1.0, 0.0).astype(BF16)
    ring[...] = dot(filt_ref[...].astype(BF16), turned, TN)

    received(ck_all.at[half], 0)
    received(cv_all.at[half], 1)
    swaps = []
    for index, ref in ((6, ck_all), (7, cv_all)):
        swap = pltpu.make_async_remote_copy(
            src_ref=ref.at[half], dst_ref=ref.at[half], send_sem=send_sem.at[index],
            recv_sem=recv_sem.at[index], device_id=(partner, me), device_id_type=MESH,
        )
        swap.start()
        swaps.append(swap)
    for swap in swaps:
        swap.wait_recv()
    received(q_all, 2)

    def fold(state, query_block, key_rows, value_rows, mask=None):
        m, l, acc = state
        s = dot(query_block, key_rows, NT)
        if mask is not None:
            s = jnp.where(mask, s, LOW)
        top = jnp.maximum(m, jnp.max(s, axis=1, keepdims=True))
        w = jnp.exp2((s - top) * scale)
        shrink = jnp.exp2((m - top) * scale)
        l = l * shrink + jnp.sum(w, axis=1, keepdims=True)
        acc = acc * shrink + dot(w.astype(BF16), value_rows, NN)
        return top, l, acc

    block = min(512, length_all)
    per_block = block // rows
    blocks = length_all // block
    ctx_total = 2 * n * half_rows
    ctx_step = 1024 if ctx_total % 1024 == 0 else ctx_total
    q_flat = q_all.reshape(length_all, width)
    k_flat = k_all.reshape(length_all, width)
    v_flat = v_all.reshape(length_all, width)
    ck_flat = ck_all.reshape(ctx_total, width)
    cv_flat = cv_all.reshape(ctx_total, width)

    def over_context(i, _):
        at = pl.ds(pl.multiple_of(i * block, block), block)
        query_block = q_flat[at, :]
        state = (
            jnp.full((block, 1), LOW, F32), jnp.zeros((block, 1), F32), jnp.zeros((block, width), F32)
        )
        for j in range(ctx_total // ctx_step):
            part = slice(j * ctx_step, (j + 1) * ctx_step)
            state = fold(state, query_block, ck_flat[part, :], cv_flat[part, :])
        m_s[at, :], l_s[at, :], acc_s[at, :] = state
        return 0

    lax.fori_loop(0, blocks, over_context, 0)

    received(k_all, 3)
    received(v_all, 4)

    o_flat = o_out.reshape(length_all, width)
    row_at = lax.broadcasted_iota(jnp.int32, (block, block), 0)
    col_at = lax.broadcasted_iota(jnp.int32, (block, block), 1)
    causal = col_at <= row_at

    def over_pair(step, _):
        low = lax.rem(step + me, blocks // 2)
        high = blocks - 1 - low

        def visit(q_index, k_index, mask=None):
            at = pl.ds(pl.multiple_of(q_index * block, block), block)
            ks = pl.ds(pl.multiple_of(k_index * block, block), block)
            state = (m_s[at, :], l_s[at, :], acc_s[at, :])
            m_s[at, :], l_s[at, :], acc_s[at, :] = fold(
                state, q_flat[at, :], k_flat[ks, :], v_flat[ks, :], mask
            )

        for t in range(blocks - 1):
            first = t < low
            visit(jnp.where(first, low, high), jnp.where(first, t, t - low))
        for index in (low, high):
            visit(index, index, causal)
            at = pl.ds(pl.multiple_of(index * block, block), block)
            o_flat[at, :] = (acc_s[at, :] / l_s[at, :]).astype(BF16)
            for r in range(per_block):
                p = index * per_block + r

                @pl.when(p != me)
                def _():
                    pltpu.make_async_remote_copy(
                        src_ref=o_out.at[p], dst_ref=o_in.at[me], send_sem=send_sem.at[8],
                        recv_sem=recv_sem.at[8], device_id=(cand, p), device_id_type=MESH,
                    ).start()
        return 0

    lax.fori_loop(0, blocks // 2, over_pair, 0)
    pltpu.make_async_copy(o_out.at[me], o_in.at[me], recv_sem.at[8]).start()

    @pl.when(me == 0)
    def _():
        def shift(j, _):
            cols = pl.ds(pl.multiple_of(j * 512, 512), 512)
            held = tail[:, cols].astype(F32)
            ext[0, :, cols] = jnp.concatenate([jnp.zeros((1, 512), F32), held], axis=0).astype(BF16)
            return 0

        lax.fori_loop(0, tail.shape[1] // 512, shift, 0)

    @pl.when(me > 0)
    def _():
        halo(me).wait_recv()

    loads[7].wait()
    valid = len_ref[0] - me * rows
    out_row = lax.broadcasted_iota(jnp.int32, (rows, 128), 0)
    out_col = lax.broadcasted_iota(jnp.int32, (rows, 128), 1)
    keep = out_row < valid
    before = out_col > out_row
    lane_group = out_col // (128 // groups_per_tile)

    def filtered(j, _):
        cols = pl.ds(pl.multiple_of(j * 128, 128), 128)
        eight = ring[pl.ds(pl.multiple_of(j * groups_per_tile, groups_per_tile), groups_per_tile), :]
        earlier = []
        current = []
        for g in range(groups_per_tile):
            spread = jnp.broadcast_to(eight[g : g + 1, :], (rows, 128))
            turns = pltpu.roll(spread, 0, 1, stride=1, stride_axis=0)
            earlier.append(jnp.where(before, turns, 0.0).astype(BF16))
            current.append(jnp.where(before, 0.0, turns).astype(BF16))
        mats = jnp.concatenate(
            [jnp.concatenate(earlier, axis=0), jnp.concatenate(current, axis=0)], axis=1
        )
        stream = jnp.concatenate([ext[0, :, cols], ext[1, :, cols]], axis=0)
        every = dot(mats, stream, NN)
        mixed = every[:rows]
        for g in range(1, groups_per_tile):
            mixed = jnp.where(lane_group == g, every[g * rows : (g + 1) * rows], mixed)
        gated = jnp.where(keep, hq[:, cols].astype(F32) * mixed, 0.0)
        hy_ref[0, :, cols] = gated.astype(BF16)
        return 0

    lax.fori_loop(0, ext.shape[2] // 128, filtered, 0)

    received(o_in, 8)
    for h in range(heads):
        wide[pl.ds(h, rows, stride=heads), :] = o_in[h].astype(F32)
    position = lax.broadcasted_iota(jnp.int32, (rows, heads, width), 0)
    att_ref[0] = jnp.where(
        position < valid, wide[...].reshape(rows, heads, width), 0.0
    ).astype(BF16)

    for index, ref in ((0, ck_out), (1, cv_out), (2, q_out), (3, k_out), (4, v_out), (8, o_out)):
        sent(ref.at[pl.ds(0, n - 1)], index)

    @pl.when(me + 1 < n)
    def _():
        halo(me + 1).wait_send()

    for swap in swaps:
        swap.wait_send()


def local(
    hyena_query, hyena_key, hyena_value, hyena_filters, context_tail,
    cont_queries, cont_keys, cont_values, context_keys, context_values, lengths,
):
    n = lax.axis_size("seq")
    _, rows, channels = hyena_key.shape
    heads, width = cont_queries.shape[2:]
    half_rows = context_keys.shape[0] // 2
    taps, groups = hyena_filters.shape
    groups_per_tile = 128 * groups // channels
    length_all = n * rows
    scale = math.log2(math.e) / math.sqrt(width)
    hbm = pl.BlockSpec(memory_space=pl.ANY)
    vmem = pl.BlockSpec(memory_space=pltpu.VMEM)
    block = pltpu.VMEM((rows, heads, width), BF16)
    per_head = pltpu.VMEM((n, rows, width), BF16)
    half_block = pltpu.VMEM((half_rows, heads, width), BF16)
    half_heads = pltpu.VMEM((n, half_rows, width), BF16)
    both_halves = pltpu.VMEM((2, n, half_rows, width), BF16)
    stream = pltpu.VMEM((rows, channels), BF16)
    return pl.pallas_call(
        functools.partial(fused, n, groups_per_tile, scale),
        out_shape=(
            jax.ShapeDtypeStruct(hyena_query.shape, BF16),
            jax.ShapeDtypeStruct(cont_queries.shape, BF16),
        ),
        in_specs=[hbm, hbm, hbm, vmem, hbm, hbm, hbm, hbm, hbm, hbm,
                  pl.BlockSpec(memory_space=pltpu.SMEM)],
        out_specs=(vmem, vmem),
        scratch_shapes=[
            stream, stream, stream,
            pltpu.VMEM(context_tail.shape, BF16),
            pltpu.VMEM((2, rows, channels), BF16),
            pltpu.VMEM((groups, taps), F32),
            block, block, block, half_block, half_block,
            pltpu.VMEM((rows * heads, width), F32),
            per_head, per_head, per_head, half_heads, half_heads,
            per_head, per_head, per_head, both_halves, both_halves,
            pltpu.VMEM((length_all, 1), F32), pltpu.VMEM((length_all, 1), F32),
            pltpu.VMEM((length_all, width), F32),
            per_head, per_head,
            pltpu.SemaphoreType.DMA((9,)), pltpu.SemaphoreType.DMA((9,)), pltpu.SemaphoreType.DMA((9,)),
        ],
        compiler_params=pltpu.CompilerParams(
            collective_id=0, has_side_effects=True, vmem_limit_bytes=63 * 2**20
        ),
        name="fused",
    )(
        hyena_query, hyena_key, hyena_value, hyena_filters, context_tail,
        cont_queries, cont_keys, cont_values, context_keys, context_values, lengths,
    )


def solution(mesh):
    placed = (
        P("cand", "seq", None), P("cand", "seq", None), P("cand", "seq", None), P(), P(),
        P("cand", "seq", None, None), P("cand", "seq", None, None), P("cand", "seq", None, None),
        P("seq", None, None), P("seq", None, None), P("cand"),
    )
    return jax.shard_map(
        local, mesh=mesh, in_specs=placed,
        out_specs=(P("cand", "seq", None), P("cand", "seq", None, None)), check_vma=False,
    )
```

time: 313 us -> 139 us (0.44)
  Pallas kernels: 0 us -> 134 us
  matrix products: 99.5 us -> 0 us
  local copies, waits for them, and re-layouts: 68.8 us -> 3.35 us
  starting transfers between devices: 51.8 us -> 0 us
  other arithmetic: 47 us -> 0 us
  waiting for transfers between devices: 35.9 us -> 0 us
  loops' own time: 5.03 us -> 0 us
    pallas_call x0 -> x1, Pallas kernels: none -> 134 us  [local(): pl.pallas_call(functools.partial(fused, n, groups_per_tile, scale), out_s...]
    dot_general x32 -> x0, matrix products: 75 us -> none  [the longest x16 39.9 us: per_block(): jnp.einsum('hqd,khd->hqk', query_block, key_rows, preferred_element_type=...]
    all_to_all x6 -> x0, starting transfers between devices: 48.4 us -> none  [the longest x1 11.1 us: local(): lax.all_to_all(context_keys, 'seq', split_axis=1, concat_axis=0, tiled=True)]
    all_to_all x6 -> x0, waiting for transfers between devices: 35.9 us -> none  [the longest x1 13.1 us: local(): lax.all_to_all(context_keys, 'seq', split_axis=1, concat_axis=0, tiled=True)]
    conv_general_dilated x1 -> x0, matrix products: 24.6 us -> none  [local(): lax.conv_general_dilated(extended, kernel, (1,), 'VALID', dimension_numbe...]
    unnamed x1 -> x0, other arithmetic: 22.6 us -> none
    reduce_sum x16 -> x0, other arithmetic: 19.5 us -> none  [merge_scores(): new_total = run_total * shrink + jnp.sum(weights, axis=-1)]
    rev x1 -> x0, local copies, waits for them, and re-layouts: 17.5 us -> none  [local(): kernel = per_channel[::-1][:, None, :]]
  transfers between devices with their start and end apart: 7 -> 0, of which waited for: 3 -> 0; matrix products, arithmetic and copies ran while one was open for 67% -> 0% of each run, Pallas kernels for 0% -> 0%
where the time goes in v1:
time: 139 us; the launch traced here: 138 us
  Pallas kernels  134 us (96%)
  local copies, waits for them, and re-layouts  3.35 us (2%)
    pallas_call x1, Pallas kernels, local(): pl.pallas_call(functools.partial(fused, n, groups_per_tile, scale), out_s...  134 us
    unnamed x4, local copies, waits for them, and re-layouts  3.35 us

profile of v1, /device:TPU:8, one launch (start us, length us, event | category | flops | bytes accessed | tf_op | source)
XLA Modules:
  0.0 138.4 jit_solution(1976910767308524483)
XLA Ops:
  1.3 133.8 %fused.1 = (bf16[1,128,4096]{2,1,0:T(8,128)(2,1)}, bf16[1,128,32,128]{3,2,1,0:T(8,128)(2,1)}) custom-call(bf16[1,128,4096]{2,1,0:T(8,128)(2,1)} %hq_hbm.1, bf16[1,128,4096]{2,1,0:T(8,128)(2,1)} %hk_hbm.1, bf16[1,128,4096]{2,1,0:T(8,128)(2,1)} %hv_hbm.1, f32[128,256]{1,0:T(8,128)} %filt_ref.1, bf16[127,4096]{1,0:T(8,128)(2,1)} %tail_hbm.1, ...), custom_call_target="tpu_custom_call" | custom-call | tf_op jit(solution)/shard_map/fused/pallas_call | solution.py:311
  135.1 0.0 copy-start
  135.1 2.4 %copy.16 = bf16[1,128,4096]{2,1,0:T(8,128)(2,1)} copy(bf16[1,128,4096]{2,1,0:T(8,128)(2,1)} %get-tuple-element.4) | data formatting | bytes 2097152
  137.5 0.0 copy-done
  137.5 1.0 copy.17
Async XLA Ops:
  135.1 2.4 %copy-start = (bf16[1,128,32,128]{3,2,1,0:T(8,128)(2,1)S(1)}, bf16[1,128,32,128]{3,2,1,0:T(8,128)(2,1)}, u32[]{:S(2)}) copy-start(bf16[1,128,32,128]{3,2,1,0:T(8,128)(2,1)} %get-tuple-element.5) | copy-start | bytes 3145732

commit v2 on v1

--- a/solution.py
+++ b/solution.py
@@ -26,7 +26,7 @@
     hq_hbm, hk_hbm, hv_hbm, filt_ref, tail_hbm, q_hbm, k_hbm, v_hbm, ck_hbm, cv_hbm, len_ref,
     hy_ref, att_ref,
     hq, hk, hv, tail, ext, ring,
-    q_in, k_in, v_in, ck_in, cv_in, wide,
+    q_in, k_in, v_in, ck_in, cv_in,
     q_out, k_out, v_out, ck_out, cv_out,
     q_all, k_all, v_all, ck_all, cv_all,
     m_s, l_s, acc_s, o_out, o_in,
@@ -66,11 +66,17 @@
     for copy in loads:
         copy.start()
 
+    perm_to = lax.broadcasted_iota(jnp.int32, (256, 256), 0)
+    perm_from = lax.broadcasted_iota(jnp.int32, (256, 256), 1)
+    swapped = (perm_to % 16) * 16 + perm_to // 16
+    perm = jnp.where(perm_from == swapped, 1.0, 0.0).astype(BF16)
+
     def by_head(src, dst):
-        count = src.shape[0]
-        wide[: count * heads, :] = src[...].astype(F32).reshape(count * heads, width)
-        for h in range(heads):
-            dst[h] = wide[pl.ds(h, count, stride=heads), :].astype(BF16)
+        for t in range(0, src.shape[0], 16):
+            for h in range(0, heads, 16):
+                tile = src[t : t + 16, h : h + 16, :].reshape(256, width)
+                turned_tile = dot(perm, tile, NN).astype(BF16)
+                dst[h : h + 16, t : t + 16, :] = turned_tile.reshape(16, 16, width)
 
     def scatter(src, dst_at, index):
         own = pltpu.make_async_copy(src.at[me], dst_at(me), recv_sem.at[index])
@@ -186,29 +192,32 @@
     received(v_all, 4)
 
     o_flat = o_out.reshape(length_all, width)
-    row_at = lax.broadcasted_iota(jnp.int32, (block, block), 0)
-    col_at = lax.broadcasted_iota(jnp.int32, (block, block), 1)
-    causal = col_at <= row_at
+    own_step = 2 * block
+    ahead = lax.broadcasted_iota(jnp.int32, (block, own_step), 1) - lax.broadcasted_iota(
+        jnp.int32, (block, own_step), 0
+    )
+
+    def over_own(index, full):
+        at = pl.ds(pl.multiple_of(index * block, block), block)
+        query_block = q_flat[at, :]
+        state = (m_s[at, :], l_s[at, :], acc_s[at, :])
+        for t in range(full + 1):
+            part = slice(t * own_step, (t + 1) * own_step)
+            mask = ahead <= index * block - full * own_step if t == full else None
+            state = fold(state, query_block, k_flat[part, :], v_flat[part, :], mask)
+        o_flat[at, :] = (state[2] / state[1]).astype(BF16)
 
     def over_pair(step, _):
         low = lax.rem(step + me, blocks // 2)
         high = blocks - 1 - low
-
-        def visit(q_index, k_index, mask=None):
-            at = pl.ds(pl.multiple_of(q_index * block, block), block)
-            ks = pl.ds(pl.multiple_of(k_index * block, block), block)
-            state = (m_s[at, :], l_s[at, :], acc_s[at, :])
-            m_s[at, :], l_s[at, :], acc_s[at, :] = fold(
-                state, q_flat[at, :], k_flat[ks, :], v_flat[ks, :], mask
-            )
-
-        for t in range(blocks - 1):
-            first = t < low
-            visit(jnp.where(first, low, high), jnp.where(first, t, t - low))
+        for g in range(blocks // 4):
+
+            @pl.when(low // 2 == g)
+            def _():
+                over_own(low, g)
+                over_own(high, blocks // 2 - 1 - g)
+
         for index in (low, high):
-            visit(index, index, causal)
-            at = pl.ds(pl.multiple_of(index * block, block), block)
-            o_flat[at, :] = (acc_s[at, :] / l_s[at, :]).astype(BF16)
             for r in range(per_block):
                 p = index * per_block + r
 
@@ -267,15 +276,15 @@
         hy_ref[0, :, cols] = gated.astype(BF16)
         return 0
 
-    lax.fori_loop(0, ext.shape[2] // 128, filtered, 0)
+    lax.fori_loop(0, ext.shape[2] // 128, filtered, 0, unroll=2)
 
     received(o_in, 8)
-    for h in range(heads):
-        wide[pl.ds(h, rows, stride=heads), :] = o_in[h].astype(F32)
-    position = lax.broadcasted_iota(jnp.int32, (rows, heads, width), 0)
-    att_ref[0] = jnp.where(
-        position < valid, wide[...].reshape(rows, heads, width), 0.0
-    ).astype(BF16)
+    row_of = lax.broadcasted_iota(jnp.int32, (256, width), 0) // 16
+    for t in range(0, rows, 16):
+        for h in range(0, heads, 16):
+            tile = o_in[h : h + 16, t : t + 16, :].reshape(256, width)
+            kept = jnp.where(row_of < valid - t, dot(perm, tile, NN), 0.0).astype(BF16)
+            att_ref[0, t : t + 16, h : h + 16, :] = kept.reshape(16, 16, width)
 
     for index, ref in ((0, ck_out), (1, cv_out), (2, q_out), (3, k_out), (4, v_out), (8, o_out)):
         sent(ref.at[pl.ds(0, n - 1)], index)
@@ -323,7 +332,6 @@
             pltpu.VMEM((2, rows, channels), BF16),
             pltpu.VMEM((groups, taps), F32),
             block, block, block, half_block, half_block,
-            pltpu.VMEM((rows * heads, width), F32),
             per_head, per_head, per_head, half_heads, half_heads,
             per_head, per_head, per_head, both_halves, both_halves,
             pltpu.VMEM((length_all, 1), F32), pltpu.VMEM((length_all, 1), F32),

time: 139 us -> 115 us (0.83)
  Pallas kernels: 134 us -> 110 us
    pallas_call x1, Pallas kernels: 134 us -> 110 us  [local(): pl.pallas_call(functools.partial(fused, n, groups_per_tile, scale), out_s...]
where the time goes in v2:
time: 115 us
  Pallas kernels  110 us (96%)
  local copies, waits for them, and re-layouts  3.35 us (3%)
  between operations  1.3 us (1%)
    pallas_call x1, Pallas kernels, local(): pl.pallas_call(functools.partial(fused, n, groups_per_tile, scale), out_s...  110 us
    unnamed x4, local copies, waits for them, and re-layouts  3.35 us

profile of v2, /device:TPU:8, one launch (start us, length us, event | category | flops | bytes accessed | tf_op | source)
XLA Modules:
  0.0 115.1 jit_solution(4034057364148943317)
XLA Ops:
  1.3 110.4 %fused.1 = (bf16[1,128,4096]{2,1,0:T(8,128)(2,1)}, bf16[1,128,32,128]{3,2,1,0:T(8,128)(2,1)}) custom-call(bf16[1,128,4096]{2,1,0:T(8,128)(2,1)} %hq_hbm.1, bf16[1,128,4096]{2,1,0:T(8,128)(2,1)} %hk_hbm.1, bf16[1,128,4096]{2,1,0:T(8,128)(2,1)} %hv_hbm.1, f32[128,256]{1,0:T(8,128)} %filt_ref.1, bf16[127,4096]{1,0:T(8,128)(2,1)} %tail_hbm.1, ...), custom_call_target="tpu_custom_call" | custom-call | tf_op jit(solution)/shard_map/fused/pallas_call | solution.py:320
  111.7 0.0 copy-start
  111.7 2.4 %copy.16 = bf16[1,128,4096]{2,1,0:T(8,128)(2,1)} copy(bf16[1,128,4096]{2,1,0:T(8,128)(2,1)} %get-tuple-element.4) | data formatting | bytes 2097152
  114.1 0.0 copy-done
  114.1 1.0 copy.17
Async XLA Ops:
  111.7 2.4 %copy-start = (bf16[1,128,32,128]{3,2,1,0:T(8,128)(2,1)S(1)}, bf16[1,128,32,128]{3,2,1,0:T(8,128)(2,1)}, u32[]{:S(2)}) copy-start(bf16[1,128,32,128]{3,2,1,0:T(8,128)(2,1)} %get-tuple-element.5) | copy-start | bytes 3145732

commit v3 on v2

--- a/solution.py
+++ b/solution.py
@@ -15,21 +15,43 @@
 NN = (((1,), (0,)), ((), ()))
 TN = (((0,), (0,)), ((), ()))
 LOW = -1e30
+RING = 4
 
 
 def dot(a, b, dims):
     return lax.dot_general(a, b, dims, preferred_element_type=F32)
+
+
+def leading_swap():
+    to = lax.broadcasted_iota(jnp.int32, (256, 256), 0)
+    source = lax.broadcasted_iota(jnp.int32, (256, 256), 1)
+    return jnp.where(source == (to % 16) * 16 + to // 16, 1.0, 0.0).astype(BF16)
+
+
+def finish(hy_ref, o_ref, len_ref, hy_out, att_ref):
+    heads, rows, width = o_ref.shape
+    total_rows = pl.num_programs(0) * rows
+    start = lax.axis_index("seq") * total_rows + pl.program_id(0) * rows
+    valid = len_ref[0] - start
+    perm = leading_swap()
+    row_of = lax.broadcasted_iota(jnp.int32, (256, width), 0) // 16
+    for t in range(0, rows, 16):
+        for h in range(0, heads, 16):
+            tile = o_ref[h : h + 16, t : t + 16, :].reshape(256, width)
+            kept = jnp.where(row_of < valid - t, dot(perm, tile, NN), 0.0).astype(BF16)
+            att_ref[0, t : t + 16, h : h + 16, :] = kept.reshape(16, 16, width)
+    hy_out[...] = hy_ref[...]
 
 
 def fused(
     n, groups_per_tile, scale,
     hq_hbm, hk_hbm, hv_hbm, filt_ref, tail_hbm, q_hbm, k_hbm, v_hbm, ck_hbm, cv_hbm, len_ref,
-    hy_ref, att_ref,
-    hq, hk, hv, tail, ext, ring,
+    hy_ref, o_in,
+    hq, hk, hv, tail, ext, ring, mats,
     q_in, k_in, v_in, ck_in, cv_in,
     q_out, k_out, v_out, ck_out, cv_out,
     q_all, k_all, v_all, ck_all, cv_all,
-    m_s, l_s, acc_s, o_out, o_in,
+    m_s, l_s, acc_s, o_out,
     load_sem, send_sem, recv_sem,
 ):
     rows, heads, width = q_in.shape
@@ -66,10 +88,7 @@
     for copy in loads:
         copy.start()
 
-    perm_to = lax.broadcasted_iota(jnp.int32, (256, 256), 0)
-    perm_from = lax.broadcasted_iota(jnp.int32, (256, 256), 1)
-    swapped = (perm_to % 16) * 16 + perm_to // 16
-    perm = jnp.where(perm_from == swapped, 1.0, 0.0).astype(BF16)
+    perm = leading_swap()
 
     def by_head(src, dst):
         for t in range(0, src.shape[0], 16):
@@ -78,19 +97,20 @@
                 turned_tile = dot(perm, tile, NN).astype(BF16)
                 dst[h : h + 16, t : t + 16, :] = turned_tile.reshape(16, 16, width)
 
+    column = me - lax.rem(me, RING)
+
     def scatter(src, dst_at, index):
         own = pltpu.make_async_copy(src.at[me], dst_at(me), recv_sem.at[index])
         own.start()
 
-        def send(i, _):
+        def send(i):
             p = lax.rem(me + i, n)
             pltpu.make_async_remote_copy(
                 src_ref=src.at[p], dst_ref=dst_at(me), send_sem=send_sem.at[index],
                 recv_sem=recv_sem.at[index], device_id=(cand, p), device_id_type=MESH,
             ).start()
-            return 0
-
-        lax.fori_loop(1, n, send, 0)
+
+        lax.fori_loop(1, n, lambda i, _: (send(i), 0)[1], 0)
 
     def received(whole, index):
         pltpu.make_async_copy(whole, whole, recv_sem.at[index]).wait()
@@ -98,6 +118,8 @@
     def sent(part, index):
         pltpu.make_async_copy(part, part, send_sem.at[index]).wait()
 
+    loads[2].wait()
+    by_head(q_in, q_out)
     loads[0].wait()
     by_head(ck_in, ck_out)
     loads[1].wait()
@@ -105,8 +127,6 @@
     pl.semaphore_wait(barrier, n)
     scatter(ck_out, lambda s: ck_all.at[half, s], 0)
     scatter(cv_out, lambda s: cv_all.at[half, s], 1)
-    loads[2].wait()
-    by_head(q_in, q_out)
     scatter(q_out, lambda s: q_all.at[s], 2)
     loads[3].wait()
     by_head(k_in, k_out)
@@ -119,15 +139,17 @@
     loads[6].wait()
     ext[1] = (hk[...].astype(F32) * hv[...].astype(F32)).astype(BF16)
 
-    def halo(to):
+    def halo(to, piece):
+        part = pl.ds(piece * 16, 16)
         return pltpu.make_async_remote_copy(
-            src_ref=ext.at[1], dst_ref=ext.at[0], send_sem=send_sem.at[5],
+            src_ref=ext.at[1, part], dst_ref=ext.at[0, part], send_sem=send_sem.at[5],
             recv_sem=recv_sem.at[5], device_id=(cand, to), device_id_type=MESH,
         )
 
     @pl.when(me + 1 < n)
     def _():
-        halo(me + 1).start()
+        for piece in range(rows // 16):
+            halo(me + 1, piece).start()
 
     loads[8].wait()
 
@@ -136,6 +158,24 @@
     turn_w = lax.broadcasted_iota(jnp.int32, (taps, taps), 1)
     turned = jnp.where((turn_s + turn_w) % taps == 0, 1.0, 0.0).astype(BF16)
     ring[...] = dot(filt_ref[...].astype(BF16), turned, TN)
+
+
+    tiles = ext.shape[2] // 128
+    out_row = lax.broadcasted_iota(jnp.int32, (rows, 128), 0)
+    out_col = lax.broadcasted_iota(jnp.int32, (rows, 128), 1)
+    before = out_col > out_row
+
+    def filter_matrices(j, _):
+        some = ring[pl.ds(pl.multiple_of(j * groups_per_tile, groups_per_tile), groups_per_tile), :]
+        for g in range(groups_per_tile):
+            line = jnp.broadcast_to(some[g : g + 1, :], (rows, 128))
+            turns = pltpu.roll(line, 0, 1, stride=1, stride_axis=0)
+            part = slice(g * rows, (g + 1) * rows)
+            mats[j, part, :128] = jnp.where(before, turns, 0.0).astype(BF16)
+            mats[j, part, 128:] = jnp.where(before, 0.0, turns).astype(BF16)
+        return 0
+
+    lax.fori_loop(0, tiles, filter_matrices, 0, unroll=2)
 
     received(ck_all.at[half], 0)
     received(cv_all.at[half], 1)
@@ -151,15 +191,18 @@
         swap.wait_recv()
     received(q_all, 2)
 
+    def spread(column):
+        return jnp.broadcast_to(column, (column.shape[0], width))
+
     def fold(state, query_block, key_rows, value_rows, mask=None):
         m, l, acc = state
         s = dot(query_block, key_rows, NT)
         if mask is not None:
             s = jnp.where(mask, s, LOW)
-        top = jnp.maximum(m, jnp.max(s, axis=1, keepdims=True))
-        w = jnp.exp2((s - top) * scale)
+        top = jnp.maximum(m, spread(jnp.max(s, axis=1, keepdims=True)))
+        w = jnp.exp2((s - jnp.concatenate([top] * (s.shape[1] // width), axis=1)) * scale)
         shrink = jnp.exp2((m - top) * scale)
-        l = l * shrink + jnp.sum(w, axis=1, keepdims=True)
+        l = l * shrink + spread(jnp.sum(w, axis=1, keepdims=True))
         acc = acc * shrink + dot(w.astype(BF16), value_rows, NN)
         return top, l, acc
 
@@ -178,7 +221,8 @@
         at = pl.ds(pl.multiple_of(i * block, block), block)
         query_block = q_flat[at, :]
         state = (
-            jnp.full((block, 1), LOW, F32), jnp.zeros((block, 1), F32), jnp.zeros((block, width), F32)
+            jnp.full((block, width), LOW, F32), jnp.zeros((block, width), F32),
+            jnp.zeros((block, width), F32),
         )
         for j in range(ctx_total // ctx_step):
             part = slice(j * ctx_step, (j + 1) * ctx_step)
@@ -208,7 +252,7 @@
         o_flat[at, :] = (state[2] / state[1]).astype(BF16)
 
     def over_pair(step, _):
-        low = lax.rem(step + me, blocks // 2)
+        low = lax.rem(step + column // RING, blocks // 2)
         high = blocks - 1 - low
         for g in range(blocks // 4):
 
@@ -244,31 +288,17 @@
 
     @pl.when(me > 0)
     def _():
-        halo(me).wait_recv()
+        received(ext.at[0], 5)
 
     loads[7].wait()
     valid = len_ref[0] - me * rows
-    out_row = lax.broadcasted_iota(jnp.int32, (rows, 128), 0)
-    out_col = lax.broadcasted_iota(jnp.int32, (rows, 128), 1)
     keep = out_row < valid
-    before = out_col > out_row
     lane_group = out_col // (128 // groups_per_tile)
 
     def filtered(j, _):
         cols = pl.ds(pl.multiple_of(j * 128, 128), 128)
-        eight = ring[pl.ds(pl.multiple_of(j * groups_per_tile, groups_per_tile), groups_per_tile), :]
-        earlier = []
-        current = []
-        for g in range(groups_per_tile):
-            spread = jnp.broadcast_to(eight[g : g + 1, :], (rows, 128))
-            turns = pltpu.roll(spread, 0, 1, stride=1, stride_axis=0)
-            earlier.append(jnp.where(before, turns, 0.0).astype(BF16))
-            current.append(jnp.where(before, 0.0, turns).astype(BF16))
-        mats = jnp.concatenate(
-            [jnp.concatenate(earlier, axis=0), jnp.concatenate(current, axis=0)], axis=1
-        )
         stream = jnp.concatenate([ext[0, :, cols], ext[1, :, cols]], axis=0)
-        every = dot(mats, stream, NN)
+        every = dot(mats[j], stream, NN)
         mixed = every[:rows]
         for g in range(1, groups_per_tile):
             mixed = jnp.where(lane_group == g, every[g * rows : (g + 1) * rows], mixed)
@@ -276,22 +306,17 @@
         hy_ref[0, :, cols] = gated.astype(BF16)
         return 0
 
-    lax.fori_loop(0, ext.shape[2] // 128, filtered, 0, unroll=2)
+    lax.fori_loop(0, tiles, filtered, 0, unroll=4)
 
     received(o_in, 8)
-    row_of = lax.broadcasted_iota(jnp.int32, (256, width), 0) // 16
-    for t in range(0, rows, 16):
-        for h in range(0, heads, 16):
-            tile = o_in[h : h + 16, t : t + 16, :].reshape(256, width)
-            kept = jnp.where(row_of < valid - t, dot(perm, tile, NN), 0.0).astype(BF16)
-            att_ref[0, t : t + 16, h : h + 16, :] = kept.reshape(16, 16, width)
-
-    for index, ref in ((0, ck_out), (1, cv_out), (2, q_out), (3, k_out), (4, v_out), (8, o_out)):
+    for index, ref in ((0, ck_out), (1, cv_out), (4, v_out), (8, o_out)):
+        sent(ref.at[pl.ds(0, n - 1)], index)
+    for index, ref in ((2, q_out), (3, k_out)):
         sent(ref.at[pl.ds(0, n - 1)], index)
 
     @pl.when(me + 1 < n)
     def _():
-        halo(me + 1).wait_send()
+        sent(ext.at[1], 5)
 
     for swap in swaps:
         swap.wait_send()
@@ -317,11 +342,11 @@
     half_heads = pltpu.VMEM((n, half_rows, width), BF16)
     both_halves = pltpu.VMEM((2, n, half_rows, width), BF16)
     stream = pltpu.VMEM((rows, channels), BF16)
-    return pl.pallas_call(
+    hyena, by_heads = pl.pallas_call(
         functools.partial(fused, n, groups_per_tile, scale),
         out_shape=(
             jax.ShapeDtypeStruct(hyena_query.shape, BF16),
-            jax.ShapeDtypeStruct(cont_queries.shape, BF16),
+            jax.ShapeDtypeStruct((n, rows, width), BF16),
         ),
         in_specs=[hbm, hbm, hbm, vmem, hbm, hbm, hbm, hbm, hbm, hbm,
                   pl.BlockSpec(memory_space=pltpu.SMEM)],
@@ -331,12 +356,13 @@
             pltpu.VMEM(context_tail.shape, BF16),
             pltpu.VMEM((2, rows, channels), BF16),
             pltpu.VMEM((groups, taps), F32),
+            pltpu.VMEM((channels // 128, groups_per_tile * rows, 2 * rows), BF16),
             block, block, block, half_block, half_block,
             per_head, per_head, per_head, half_heads, half_heads,
             per_head, per_head, per_head, both_halves, both_halves,
-            pltpu.VMEM((length_all, 1), F32), pltpu.VMEM((length_all, 1), F32),
+            pltpu.VMEM((length_all, width), F32), pltpu.VMEM((length_all, width), F32),
             pltpu.VMEM((length_all, width), F32),
-            per_head, per_head,
+            per_head,
             pltpu.SemaphoreType.DMA((9,)), pltpu.SemaphoreType.DMA((9,)), pltpu.SemaphoreType.DMA((9,)),
         ],
         compiler_params=pltpu.CompilerParams(
@@ -347,6 +373,20 @@
         hyena_query, hyena_key, hyena_value, hyena_filters, context_tail,
         cont_queries, cont_keys, cont_values, context_keys, context_values, lengths,
     )
+    part = rows // 2
+    hy_spec = pl.BlockSpec((1, part, channels), lambda i: (0, i, 0))
+    return pl.pallas_call(
+        finish,
+        grid=(rows // part,),
+        out_shape=(
+            jax.ShapeDtypeStruct(hyena_query.shape, BF16),
+            jax.ShapeDtypeStruct(cont_queries.shape, BF16),
+        ),
+        in_specs=[hy_spec, pl.BlockSpec((n, part, width), lambda i: (0, i, 0)),
+                  pl.BlockSpec(memory_space=pltpu.SMEM)],
+        out_specs=(hy_spec, pl.BlockSpec((1, part, heads, width), lambda i: (0, i, 0, 0))),
+        name="finish",
+    )(hyena, by_heads, lengths)
 
 
 def solution(mesh):

time: 115 us -> 103 us (0.90)
  Pallas kernels: 110 us -> 102 us
  local copies, waits for them, and re-layouts: 3.35 us -> 0 us
    pallas_call x1, Pallas kernels: 110 us -> 98.6 us  [local(): pl.pallas_call(functools.partial(fused, n, groups_per_tile, scale), out_s...]
    unnamed x4 -> x0, local copies, waits for them, and re-layouts: 3.35 us -> none
    pallas_call x0 -> x1, Pallas kernels: none -> 3.02 us  [local(): pl.pallas_call(finish, grid=(rows // part,), out_shape=(jax.ShapeDtypeStr...]
where the time goes in v3:
time: 103 us
  Pallas kernels  102 us (99%)
  between operations  1.29 us (1%)
    pallas_call x1, Pallas kernels, local(): pl.pallas_call(functools.partial(fused, n, groups_per_tile, scale), out_s...  98.6 us
    pallas_call x1, Pallas kernels, local(): pl.pallas_call(finish, grid=(rows // part,), out_shape=(jax.ShapeDtypeStr...  3.02 us

profile of v3, /device:TPU:8, one launch (start us, length us, event | category | flops | bytes accessed | tf_op | source)
XLA Modules:
  0.0 103.0 jit_solution(1956700700847903646)
XLA Ops:
  1.3 98.6 %fused.1 = (bf16[1,128,4096]{2,1,0:T(8,128)(2,1)}, bf16[32,128,128]{2,1,0:T(8,128)(2,1)}) custom-call(bf16[1,128,4096]{2,1,0:T(8,128)(2,1)} %hq_hbm.1, bf16[1,128,4096]{2,1,0:T(8,128)(2,1)} %hk_hbm.1, bf16[1,128,4096]{2,1,0:T(8,128)(2,1)} %hv_hbm.1, f32[128,256]{1,0:T(8,128)} %filt_ref.1, bf16[127,4096]{1,0:T(8,128)(2,1)} %tail_hbm.1, ...), custom_call_target="tpu_custom_call" | custom-call | tf_op jit(solution)/shard_map/fused/pallas_call | solution.py:345
  99.9 3.0 %finish.1 = (bf16[1,128,4096]{2,1,0:T(8,128)(2,1)}, bf16[1,128,32,128]{3,2,1,0:T(8,128)(2,1)}) custom-call(bf16[1,128,4096]{2,1,0:T(8,128)(2,1)} %get-tuple-element.4.hy_ref, bf16[32,128,128]{2,1,0:T(8,128)(2,1)} %get-tuple-element.5.o_ref, s32[1]{0:T(128)S(6)} %copy.13.len_ref), custom_call_target="tpu_custom_call" | custom-call | tf_op jit(solution)/shard_map/finish/pallas_call | solution.py:378

commit v4 on v3

--- a/solution.py
+++ b/solution.py
@@ -46,8 +46,8 @@
 def fused(
     n, groups_per_tile, scale,
     hq_hbm, hk_hbm, hv_hbm, filt_ref, tail_hbm, q_hbm, k_hbm, v_hbm, ck_hbm, cv_hbm, len_ref,
-    hy_ref, o_in,
-    hq, hk, hv, tail, ext, ring, mats,
+    hy_hbm, o_in,
+    hq, hk, hv, hy, tail, ext, ring, mats,
     q_in, k_in, v_in, ck_in, cv_in,
     q_out, k_out, v_out, ck_out, cv_out,
     q_all, k_all, v_all, ck_all, cv_all,
@@ -118,8 +118,6 @@
     def sent(part, index):
         pltpu.make_async_copy(part, part, send_sem.at[index]).wait()
 
-    loads[2].wait()
-    by_head(q_in, q_out)
     loads[0].wait()
     by_head(ck_in, ck_out)
     loads[1].wait()
@@ -127,6 +125,8 @@
     pl.semaphore_wait(barrier, n)
     scatter(ck_out, lambda s: ck_all.at[half, s], 0)
     scatter(cv_out, lambda s: cv_all.at[half, s], 1)
+    loads[2].wait()
+    by_head(q_in, q_out)
     scatter(q_out, lambda s: q_all.at[s], 2)
     loads[3].wait()
     by_head(k_in, k_out)
@@ -303,12 +303,16 @@
         for g in range(1, groups_per_tile):
             mixed = jnp.where(lane_group == g, every[g * rows : (g + 1) * rows], mixed)
         gated = jnp.where(keep, hq[:, cols].astype(F32) * mixed, 0.0)
-        hy_ref[0, :, cols] = gated.astype(BF16)
+        hy[:, cols] = gated.astype(BF16)
         return 0
 
     lax.fori_loop(0, tiles, filtered, 0, unroll=4)
 
+    store = pltpu.make_async_copy(hy, hy_hbm.at[0], load_sem.at[7])
+    store.start()
+
     received(o_in, 8)
+    store.wait()
     for index, ref in ((0, ck_out), (1, cv_out), (4, v_out), (8, o_out)):
         sent(ref.at[pl.ds(0, n - 1)], index)
     for index, ref in ((2, q_out), (3, k_out)):
@@ -350,9 +354,9 @@
         ),
         in_specs=[hbm, hbm, hbm, vmem, hbm, hbm, hbm, hbm, hbm, hbm,
                   pl.BlockSpec(memory_space=pltpu.SMEM)],
-        out_specs=(vmem, vmem),
+        out_specs=(hbm, hbm),
         scratch_shapes=[
-            stream, stream, stream,
+            stream, stream, stream, stream,
             pltpu.VMEM(context_tail.shape, BF16),
             pltpu.VMEM((2, rows, channels), BF16),
             pltpu.VMEM((groups, taps), F32),

time: 103 us -> 102 us (level)
    pallas_call x1, Pallas kernels: 98.6 us -> 97.6 us  [local(): pl.pallas_call(functools.partial(fused, n, groups_per_tile, scale), out_s...]
where the time goes in v4:
time: 102 us
  Pallas kernels  101 us (99%)
  between operations  1.29 us (1%)
    pallas_call x1, Pallas kernels, local(): pl.pallas_call(functools.partial(fused, n, groups_per_tile, scale), out_s...  97.6 us
    pallas_call x1, Pallas kernels, local(): pl.pallas_call(finish, grid=(rows // part,), out_shape=(jax.ShapeDtypeStr...  3.02 us

profile of v4, /device:TPU:8, one launch (start us, length us, event | category | flops | bytes accessed | tf_op | source)
XLA Modules:
  0.0 101.9 jit_solution(11651789637953140344)
XLA Ops:
  1.3 97.6 %fused.1 = (bf16[1,128,4096]{2,1,0:T(8,128)(2,1)}, bf16[32,128,128]{2,1,0:T(8,128)(2,1)}) custom-call(bf16[1,128,4096]{2,1,0:T(8,128)(2,1)} %hq_hbm.1, bf16[1,128,4096]{2,1,0:T(8,128)(2,1)} %hk_hbm.1, bf16[1,128,4096]{2,1,0:T(8,128)(2,1)} %hv_hbm.1, f32[128,256]{1,0:T(8,128)} %filt_ref.1, bf16[127,4096]{1,0:T(8,128)(2,1)} %tail_hbm.1, ...), custom_call_target="tpu_custom_call" | custom-call | tf_op jit(solution)/shard_map/fused/pallas_call | solution.py:349
  98.9 3.0 %finish.1 = (bf16[1,128,4096]{2,1,0:T(8,128)(2,1)}, bf16[1,128,32,128]{3,2,1,0:T(8,128)(2,1)}) custom-call(bf16[1,128,4096]{2,1,0:T(8,128)(2,1)} %get-tuple-element.4.hy_ref, bf16[32,128,128]{2,1,0:T(8,128)(2,1)} %get-tuple-element.5.o_ref, s32[1]{0:T(128)S(6)} %copy.13.len_ref), custom_call_target="tpu_custom_call" | custom-call | tf_op jit(solution)/shard_map/finish/pallas_call | solution.py:382

commit v5 on v4

--- a/solution.py
+++ b/solution.py
@@ -254,14 +254,13 @@
     def over_pair(step, _):
         low = lax.rem(step + column // RING, blocks // 2)
         high = blocks - 1 - low
-        for g in range(blocks // 4):
-
-            @pl.when(low // 2 == g)
-            def _():
-                over_own(low, g)
-                over_own(high, blocks // 2 - 1 - g)
-
-        for index in (low, high):
+        for index, of_low in ((low, True), (high, False)):
+            for g in range(blocks // 4):
+
+                @pl.when(low // 2 == g)
+                def _():
+                    over_own(index, g if of_low else blocks // 2 - 1 - g)
+
             for r in range(per_block):
                 p = index * per_block + r
 

time: 102 us -> 104 us (1.020)
    pallas_call x1, Pallas kernels: 97.6 us -> 99.3 us  [local(): pl.pallas_call(functools.partial(fused, n, groups_per_tile, scale), out_s...]
where the time goes in v5:
time: 104 us
  Pallas kernels  102 us (98%)
  between operations  1.29 us (1%)
    pallas_call x1, Pallas kernels, local(): pl.pallas_call(functools.partial(fused, n, groups_per_tile, scale), out_s...  99.3 us
    pallas_call x1, Pallas kernels, local(): pl.pallas_call(finish, grid=(rows // part,), out_shape=(jax.ShapeDtypeStr...  3.02 us

profile of v5, /device:TPU:8, one launch (start us, length us, event | category | flops | bytes accessed | tf_op | source)
XLA Modules:
  0.0 103.6 jit_solution(11133655829684479629)
XLA Ops:
  1.3 99.3 %fused.1 = (bf16[1,128,4096]{2,1,0:T(8,128)(2,1)}, bf16[32,128,128]{2,1,0:T(8,128)(2,1)}) custom-call(bf16[1,128,4096]{2,1,0:T(8,128)(2,1)} %hq_hbm.1, bf16[1,128,4096]{2,1,0:T(8,128)(2,1)} %hk_hbm.1, bf16[1,128,4096]{2,1,0:T(8,128)(2,1)} %hv_hbm.1, f32[128,256]{1,0:T(8,128)} %filt_ref.1, bf16[127,4096]{1,0:T(8,128)(2,1)} %tail_hbm.1, ...), custom_call_target="tpu_custom_call" | custom-call | tf_op jit(solution)/shard_map/fused/pallas_call | solution.py:348
  100.6 3.0 %finish.1 = (bf16[1,128,4096]{2,1,0:T(8,128)(2,1)}, bf16[1,128,32,128]{3,2,1,0:T(8,128)(2,1)}) custom-call(bf16[1,128,4096]{2,1,0:T(8,128)(2,1)} %get-tuple-element.4.hy_ref, bf16[32,128,128]{2,1,0:T(8,128)(2,1)} %get-tuple-element.5.o_ref, s32[1]{0:T(128)S(6)} %copy.13.len_ref), custom_call_target="tpu_custom_call" | custom-call | tf_op jit(solution)/shard_map/finish/pallas_call | solution.py:381
